TPU v7x, 128 devices: a whole 4x4x4 slice. The times are simulated.
128 devices in a mesh: gx: 8 (over y, core), gy: 16 (over z, x).
Axes of the slice: x: 4, y: 4, z: 4, core: 2. Of those that a mesh axis runs over, the one named last changes fastest.
Arguments:
- right_side: float32 [128, 512, 256], P('gx', 'gy'), may hold values from -30 to 30
- start_field: float32 [128, 512, 256], P('gx', 'gy'), may hold values from -1.8 to 1.8
- coef: float32 [128, 512, 256], P('gx', 'gy'), may hold values from 0.5 to 2
- deflation: float32 [8, 128, 512, 256], P(None, 'gx', 'gy'), may hold values from -9 to 9
Outputs:
- solution: float32 [128, 512, 256], P('gx', 'gy')
- residual: float32 [128, 512, 256], P('gx', 'gy')
- direction: float32 [128, 512, 256], P('gx', 'gy')
All inputs are finite; a program needn't handle non-finite values.
Results may differ from a plain program's by a relative error of at most 0.0003.
Values sent between devices are 32-bit elements; how exact they have to be, the bound alone decides.
A program may use at most 192 MiB of HBM per device.

v0:
```python
import jax
import jax.numpy as jnp
from jax import lax
from jax.sharding import PartitionSpec as P

ITERS = 2
highest = lax.Precision.HIGHEST


def extended(cells, sides, width):
    for axis, dim in sides:
        count = lax.axis_size(axis)
        ends = count - 1
        head = lax.slice_in_dim(cells, 0, width, axis=dim)
        tail = lax.slice_in_dim(cells, cells.shape[dim] - width, cells.shape[dim], axis=dim)
        cells = jnp.concatenate(
            [
                lax.ppermute(tail, axis, [(i, (i + 1) % count) for i in range(ends)]),
                cells,
                lax.ppermute(head, axis, [((i + 1) % count, i) for i in range(ends)]),
            ],
            axis=dim,
        )
    return cells


def face_coef(padded, along):
    length = padded.shape[along]
    lower_side = lax.slice_in_dim(padded, 0, length - 1, axis=along)
    upper_side = lax.slice_in_dim(padded, 1, length, axis=along)
    inside = (lower_side > 0.0) & (upper_side > 0.0)
    summed = lower_side + upper_side
    return jnp.where(inside, 2.0 * lower_side * upper_side / summed, summed)


def block_operate(vectors, face_rows, face_cols, face_depth, diagonal):
    padded = jnp.pad(vectors, ((0, 0), (1, 1), (1, 1), (1, 1)))
    beside = face_rows[1:] * padded[:, 2:, 1:-1, 1:-1] + face_rows[:-1] * padded[:, :-2, 1:-1, 1:-1]
    beside = (
        beside
        + face_cols[:, 1:] * padded[:, 1:-1, 2:, 1:-1]
        + face_cols[:, :-1] * padded[:, 1:-1, :-2, 1:-1]
    )
    beside = (
        beside
        + face_depth[:, :, 1:] * padded[:, 1:-1, 1:-1, 2:]
        + face_depth[:, :, :-1] * padded[:, 1:-1, 1:-1, :-2]
    )
    return diagonal * vectors - beside


def face_product(lower_part, weights, upper_part):
    return -jnp.einsum("kab,lab->kl", lower_part * weights, upper_part, precision=highest)


def place(selector, blocks):
    return selector.astype(jnp.float32)[:, None, :, None] * blocks[:, :, None, :]


def block_masks(block_count, across):
    positions = jnp.arange(block_count, dtype=jnp.int32)
    row_ids = positions[:, None]
    col_ids = positions[None, :]
    self_mask = row_ids == col_ids
    below_rows = col_ids == row_ids - across
    below_cols = (col_ids == row_ids - 1) & (row_ids % across != 0)
    above_rows = col_ids == row_ids + across
    above_cols = (col_ids == row_ids + 1) & (col_ids % across != 0)
    return (self_mask, below_rows, below_cols, above_rows, above_cols)


def per_device(right_side, start_field, coef, deflation):
    num_vectors = deflation.shape[0]
    across = lax.axis_size("gy")
    block_count = lax.axis_size("gx") * across
    own_block = lax.axis_index("gx") * across + lax.axis_index("gy")
    padded = extended(coef, (("gx", 0), ("gy", 1)), 1)
    face_rows = face_coef(padded[:, 1:-1], 0)
    face_cols = face_coef(padded[1:-1], 1)
    face_depth = face_coef(jnp.pad(coef, ((0, 0), (0, 0), (1, 1))), 2)
    diagonal = face_rows[1:] + face_rows[:-1] + face_cols[:, 1:] + face_cols[:, :-1]
    diagonal = diagonal + face_depth[:, :, 1:] + face_depth[:, :, :-1]

    def apply_operator(values):
        rimmed_values = extended(values, (("gx", 0), ("gy", 1)), 1)
        depth_padded = jnp.pad(values, ((0, 0), (0, 0), (1, 1)))
        beside = face_rows[1:] * rimmed_values[2:, 1:-1] + face_rows[:-1] * rimmed_values[:-2, 1:-1]
        beside = (
            beside
            + face_cols[:, 1:] * rimmed_values[1:-1, 2:]
            + face_cols[:, :-1] * rimmed_values[1:-1, :-2]
        )
        beside = (
            beside
            + face_depth[:, :, 1:] * depth_padded[:, :, 2:]
            + face_depth[:, :, :-1] * depth_padded[:, :, :-2]
        )
        return diagonal * values - beside

    acted_on = block_operate(deflation, face_rows, face_cols, face_depth, diagonal)
    diag_block = jnp.einsum("kxyz,lxyz->kl", deflation, acted_on, precision=highest)
    rimmed = extended(deflation, (("gx", 1), ("gy", 2)), 1)
    below_rows = face_product(deflation[:, 0], face_rows[0], rimmed[:, 0, 1:-1])
    below_cols = face_product(deflation[:, :, 0], face_cols[:, 0], rimmed[:, 1:-1, 0])
    above_rows = face_product(deflation[:, -1], face_rows[-1], rimmed[:, -1, 1:-1])
    above_cols = face_product(deflation[:, :, -1], face_cols[:, -1], rimmed[:, 1:-1, -1])
    blocks = jnp.stack([diag_block, below_rows, below_cols, above_rows, above_cols])[None]
    gathered = lax.all_gather(blocks, ("gx", "gy"), axis=0, tiled=True)
    self_mask, mask_below_rows, mask_below_cols, mask_above_rows, mask_above_cols = block_masks(
        block_count, across
    )
    matrix = (
        place(self_mask, gathered[:, 0])
        + place(mask_below_rows, gathered[:, 1])
        + place(mask_below_cols, gathered[:, 2])
    )
    matrix = (
        matrix + place(mask_above_rows, gathered[:, 3]) + place(mask_above_cols, gathered[:, 4])
    )
    matrix = matrix.reshape(block_count * num_vectors, block_count * num_vectors)
    factor = jnp.linalg.cholesky(matrix)

    def solve_coarse(gathered_rows):
        flattened = gathered_rows.reshape(-1)
        solved = jax.scipy.linalg.cho_solve((factor, True), flattened)
        return lax.dynamic_slice_in_dim(solved, own_block * num_vectors, num_vectors)

    def restrict(values):
        return jnp.einsum("kxyz,xyz->k", deflation, values, precision=highest)

    def prolong(coarse_values):
        return jnp.einsum("kxyz,k->xyz", deflation, coarse_values, precision=highest)

    def coarse_plain(values):
        gathered_rows = lax.all_gather(restrict(values)[None], ("gx", "gy"), axis=0, tiled=True)
        return prolong(solve_coarse(gathered_rows))

    def coarse_with(values, residual_now, precond_now):
        inner_sum = lax.psum(jnp.sum(residual_now * precond_now), ("gx", "gy"))
        return (coarse_plain(values), inner_sum)

    solution = start_field + coarse_plain(right_side - apply_operator(start_field))
    residual = right_side - apply_operator(solution)
    precond = residual / diagonal
    correction, inner_now = coarse_with(apply_operator(precond), residual, precond)
    direction = precond - correction
    for iteration in range(ITERS):
        applied = apply_operator(direction)
        step_size = inner_now / lax.psum(jnp.sum(direction * applied), ("gx", "gy"))
        solution = solution + step_size * direction
        residual = residual - step_size * applied
        precond = residual / diagonal
        correction, inner_next = coarse_with(apply_operator(precond), residual, precond)
        direction = precond + inner_next / inner_now * direction - correction
        inner_now = inner_next
    return (solution, residual, direction)


def solution(mesh):
    placed = (
        P("gx", "gy", None),
        P("gx", "gy", None),
        P("gx", "gy", None),
        P(None, "gx", "gy", None),
    )
    return jax.shard_map(
        per_device,
        mesh=mesh,
        in_specs=placed,
        out_specs=(P("gx", "gy", None), P("gx", "gy", None), P("gx", "gy", None)),
        check_vma=False,
    )
```

profile of v0, /device:TPU:1, one launch (start us, length us, event | category | flops | bytes accessed | tf_op | source)
XLA Modules:
  0.0 1258.0 jit_solution(12469603402888341044)
XLA Ops:
  2.1 4.6 collective-permute-start
  13.2 3.9 collective-permute-start.9
  17.1 5.5 copy.75
  31.4 4.5 copy.77
  46.8 3.1 collective-permute-start.2
  56.7 4.6 collective-permute-start.11
  68.2 14.7 %fusion.6 = f32[8,16,32,256]{3,2,1,0:T(8,128)} fusion(f32[8,16,32,256]{3,2,1,0:T(8,128)} %param.9, f32[16,32,256]{2,1,0:T(8,128)} %copy.73, f32[16,32,256]{2,1,0:T(8,128)} %copy.72, f32[16,32,256]{2,1,0:T(8,128)} %copy.71, f32[16,32,256]{2,1,0:T(8,128)} %copy.70, f32[16,32,256]{2,1,0:T(8,128)} %copy.69, f32[16,32,256]{2,1,0:T(8,128)} %copy.68, ...), kind=kLoop, calls=%fused_computation.16 | loop fusion | flops 13631488 | bytes 12058624 | tf_op jit(solution)/shard_map/sub | solution.py:49
  82.9 15.8 %fusion.15 = f32[8,8]{0,1:T(8,128)} fusion(f32[8,16,32,256]{3,2,1,0:T(8,128)} %fusion.6, f32[8,16,32,256]{3,2,1,0:T(8,128)} %param.9), kind=kOutput, calls=%fused_computation.42 | convolution fusion | flops 100663296 | bytes 8388864 | tf_op jit(solution)/shard_map/kxyz,lxyz->kl/dot_general | solution.py:101
  100.1 12.9 %convolution_bitcast_fusion.23 = f32[8]{0:T(128)} fusion(f32[16,32,256,1]{2,0,1,3:T(8,128)S(1)} %copy-done.28, f32[8,16,32,256]{3,2,1,0:T(8,128)} %param.9), kind=kOutput, calls=%fused_computation.78 | convolution fusion | flops 12582912 | bytes 4718624 | tf_op jit(solution)/shard_map/kxyz,xyz->k/dot_general | solution.py:129
  113.9 72.3 %all-reduce.10 = f32[1024]{0:T(1024)} all-reduce(f32[1024]{0:T(1024)S(1)} %dynamic-update-slice.50), channel_id=3, replica_groups=mesh['gx'=8,'gy'=16] {'gx','gy'}, use_global_device_ids=true, to_apply=%add.10 | all-reduce | flops 1024 | bytes 8192
  196.5 69.1 %all-gather = f32[640,8,8]{2,1,0:T(8,128)S(1)} all-gather(f32[5,8,8]{2,1,0:T(8,128)S(1)} %fusion.20), channel_id=2, replica_groups=mesh['gx'=8,'gy'=16] {'gx','gy'}, dimensions={0}, use_global_device_ids=true | all-gather | bytes 165120 | tf_op jit(solution)/shard_map/all_gather | solution.py:108
  265.9 31.1 %multiply_add_fusion = f32[128,8,128,8]{3,2,1,0:T(8,128)} fusion(f32[128,8,8]{2,1,0:T(8,128)S(1)} %get-tuple-element.76, f32[128,128]{1,0:T(8,128)S(1)} %copy-done.36, f32[128,8,8]{2,1,0:T(8,128)S(1)} %get-tuple-element.77, f32[128,128]{1,0:T(8,128)S(1)} %copy-done.34, f32[128,8,8]{2,1,0:T(8,128)S(1)} %get-tuple-element.78, f32[128,128]{1,0:T(8,128)S(1)} %copy-done.35, ...), kind=kLoop, calls=%fused_computation.2 | loop fusion | flops 9437184 | bytes 4685824 | tf_op jit(solution)/shard_map/add | solution.py:118
  297.0 48.3 %reshape.508 = f32[1024,1024]{1,0:T(8,128)} reshape(f32[128,8,128,8]{3,2,1,0:T(8,128)} %multiply_add_fusion) | data formatting | bytes 8388608 | tf_op jit(solution)/shard_map/add | solution.py:118
  345.3 5.5 copy.85
  350.8 4.4 fusion.12
  357.3 11.7 cholesky.226
  371.6 9.8 custom-call.64
  385.4 11.9 cholesky.247
  399.2 9.8 custom-call.65
  412.3 11.7 cholesky.474
  425.4 9.8 custom-call.66
  438.7 12.1 cholesky.493
  452.1 9.8 custom-call.67
  465.3 11.7 cholesky.512
  478.4 9.9 custom-call.68
  491.6 11.7 cholesky.532
  504.6 9.8 custom-call.69
  517.5 11.9 cholesky.552
  530.7 9.8 custom-call.70
  543.2 11.7 cholesky.570
  561.4 4.9 select_select_fusion
  566.3 28.1 %while.8 = (s32[]{:T(128)}, f32[1024,1024]{1,0:T(8,128)}, s32[8,2]{0,1:T(2,128)S(1)}, f32[8,128,128]{2,1,0:T(8,128)}, s32[]{:T(128)}) while((s32[]{:T(128)}, f32[1024,1024]{1,0:T(8,128)}, s32[8,2]{0,1:T(2,128)S(1)}, f32[8,128,128]{2,1,0:T(8,128)}, s32[]{:T(128)}) %tuple.176), condition=%wide.while_cond, body=%wide.while_body.sunk | while | flops 2 | bytes 132705 | solution.py:125
  566.8 2.9 bitcast_dynamic-update-slice_fusion.2
  570.4 2.9 bitcast_dynamic-update-slice_fusion.2
  573.9 2.9 bitcast_dynamic-update-slice_fusion.2
  577.4 2.9 bitcast_dynamic-update-slice_fusion.2
  580.9 2.9 bitcast_dynamic-update-slice_fusion.2
  584.4 2.9 bitcast_dynamic-update-slice_fusion.2
  587.9 2.9 bitcast_dynamic-update-slice_fusion.2
  594.3 79.8 %custom-call.74 = f32[8,128,128]{1,2,0:T(8,128)S(1)} custom-call(f32[8,128,128]{2,1,0:T(8,128)} %get-tuple-element.30), custom_call_target="InvertDiagBlocksLowerTriangular" | custom-call | tf_op jit(solution)/shard_map/jit(_cho_solve)/triangular_solve | solution.py:125
  695.3 5.2 fusion.497
  701.2 3.3 collective-permute-start.12
  709.1 4.0 collective-permute-start.15
  716.3 3.0 collective-permute-start.16
  719.3 4.3 collective-permute-start.17
  725.9 4.7 collective-permute-start.19
  732.1 10.9 convolution_bitcast_fusion.18
  743.2 69.9 %all-reduce.11 = f32[1024]{0:T(1024)S(1)} all-reduce(f32[1024]{0:T(1024)S(1)} %dynamic-update-slice.51), channel_id=4, replica_groups=mesh['gx'=8,'gy'=16] {'gx','gy'}, use_global_device_ids=true, to_apply=%add.11 | all-reduce | flops 1024 | bytes 8192
  834.1 5.2 fusion.495
  842.3 3.1 collective-permute-start.21
  847.8 4.0 collective-permute-start.23
  854.7 68.3 %all-reduce.16 = (f32[]{:T(128)}, f32[]{:T(128)}) all-reduce(f32[]{:T(128)} %get-tuple-element.64, f32[]{:T(128)} %get-tuple-element.62), channel_id=1, replica_groups=mesh['gx'=8,'gy'=16] {'gx','gy'}, use_global_device_ids=true, to_apply=%region_17.19 | all-reduce | flops 2 | bytes 16 | tf_op jit(solution)/shard_map/psum | solution.py:139
  924.2 2.9 multiply_reduce_fusion.2
  935.0 4.4 collective-permute-start.27
  940.5 10.6 convolution_bitcast_fusion.13
  951.3 68.2 %all-reduce.15 = (f32[1024]{0:T(1024)S(1)}, f32[]{:T(128)}) all-reduce(f32[1024]{0:T(1024)S(1)} %dynamic-update-slice.52, f32[]{:T(128)} %get-tuple-element.59), channel_id=5, replica_groups=mesh['gx'=8,'gy'=16] {'gx','gy'}, use_global_device_ids=true, to_apply=%add.12 | all-reduce | flops 1025 | bytes 8200
  1042.1 5.2 fusion.493
  1050.5 2.9 collective-permute-start.29
  1055.6 4.0 collective-permute-start.31
  1062.6 68.1 %psum.38 = f32[]{:T(128)} all-reduce(f32[]{:T(128)} %get-tuple-element.57), channel_id=1, replica_groups=mesh['gx'=8,'gy'=16] {'gx','gy'}, use_global_device_ids=true, to_apply=%region_23.25 | all-reduce | flops 1 | bytes 8 | tf_op jit(solution)/shard_map/psum | solution.py:149
  1142.3 4.2 collective-permute-start.35
  1148.1 10.6 convolution_bitcast_fusion.8
  1159.0 68.0 %all-reduce.14 = (f32[1024]{0:T(1024)S(1)}, f32[]{:T(128)}) all-reduce(f32[1024]{0:T(1024)S(1)} %dynamic-update-slice.53, f32[]{:T(128)} %get-tuple-element.54), channel_id=6, replica_groups=mesh['gx'=8,'gy'=16] {'gx','gy'}, use_global_device_ids=true, to_apply=%add.13 | all-reduce | flops 1025 | bytes 8200
  1249.6 5.2 fusion.491
  (490 shorter events, 236.1 us)
Async XLA Ops:
  2.1 42.5 %collective-permute-start = (f32[1,32,256]{2,0,1:T(1,128)}, f32[1,32,256]{2,0,1:T(1,128)}, u32[]{:S(2)}, u32[]{:S(2)}) collective-permute-start(f32[1,32,256]{2,0,1:T(1,128)} %copy.61), channel_id=1, source_target_pairs={{0,16},{16,32},{32,48},{48,64},{64,80},{80,96},{96,112},{1,17},{17... | collective-permute-start | bytes 98312 | tf_op jit(solution)/shard_map/ppermute | solution.py:18
  7.3 33.5 %collective-permute-start.1 = (f32[1,32,256]{2,0,1:T(1,128)}, f32[1,32,256]{2,0,1:T(1,128)}, u32[]{:S(2)}, u32[]{:S(2)}) collective-permute-start(f32[1,32,256]{2,0,1:T(1,128)} %copy.63), channel_id=1, source_target_pairs={{16,0},{32,16},{48,32},{64,48},{80,64},{96,80},{112,96},{17,1},{33... | collective-permute-start | bytes 98312 | tf_op jit(solution)/shard_map/ppermute | solution.py:20
  10.6 39.3 %collective-permute-start.8 = (f32[1,32,256]{2,0,1:T(1,128)}, f32[1,32,256]{2,0,1:T(1,128)}, u32[]{:S(2)}, u32[]{:S(2)}) collective-permute-start(f32[1,32,256]{2,0,1:T(1,128)} %copy.87), channel_id=1, source_target_pairs={{16,0},{32,16},{48,32},{64,48},{80,64},{96,80},{112,96},{17,1},{33... | collective-permute-start | bytes 98312 | tf_op jit(solution)/shard_map/ppermute | solution.py:20
  13.2 38.1 %collective-permute-start.9 = (f32[1,32,256]{2,0,1:T(1,128)}, f32[1,32,256]{2,0,1:T(1,128)}, u32[]{:S(2)}, u32[]{:S(2)}) collective-permute-start(f32[1,32,256]{2,0,1:T(1,128)} %copy.89), channel_id=1, source_target_pairs={{0,16},{16,32},{32,48},{48,64},{64,80},{80,96},{96,112},{1,17},{17... | collective-permute-start | bytes 98312 | tf_op jit(solution)/shard_map/ppermute | solution.py:18
  23.4 163.6 %collective-permute-start.4 = (f32[8,1,32,256]{3,0,2,1:T(8,128)}, f32[8,1,32,256]{3,0,2,1:T(8,128)S(1)}, u32[]{:S(2)}, u32[]{:S(2)}) collective-permute-start(f32[8,1,32,256]{3,0,2,1:T(8,128)} %slice.817), channel_id=1, source_target_pairs={{0,16},{16,32},{32,48},{48,64},{64,80},{80,96},{96,112},{1,17},{17... | collective-permute-start | bytes 786440 | tf_op jit(solution)/shard_map/ppermute | solution.py:18
  40.8 146.1 %collective-permute-start.5 = (f32[8,1,32,256]{3,0,1,2:T(8,128)}, f32[8,1,32,256]{3,0,1,2:T(8,128)}, u32[]{:S(2)}, u32[]{:S(2)}) collective-permute-start(f32[8,1,32,256]{3,0,1,2:T(8,128)} %slice.815), channel_id=1, source_target_pairs={{16,0},{32,16},{48,32},{64,48},{80,64},{96,80},{112,96},{17,1},{33... | collective-permute-start | bytes 786440 | tf_op jit(solution)/shard_map/ppermute | solution.py:20
  46.0 17.1 %copy-start.26 = (f32[16,32,256]{2,1,0:T(8,128)S(1)}, f32[16,32,256]{2,1,0:T(8,128)}, u32[]{:S(2)}) copy-start(f32[16,32,256]{2,1,0:T(8,128)} %param.6) | copy-start | bytes 1572868
  46.8 9.9 collective-permute-start.2
  50.0 11.3 collective-permute-start.3
  51.9 11.2 collective-permute-start.10
  56.7 6.4 collective-permute-start.11
  82.9 17.2 %copy-start.28 = (f32[16,32,256,1]{2,0,1,3:T(8,128)S(1)}, f32[16,32,256,1]{2,0,1,3:T(8,128)}, u32[]{:S(2)}) copy-start(f32[16,32,256,1]{2,0,1,3:T(8,128)} %get-tuple-element.67) | copy-start | bytes 1572868
  113.0 77.6 %copy-start.38 = (f32[1,32,256]{2,1,0:T(8,128)S(1)}, f32[1,32,256]{2,1,0:T(8,128)}, u32[]{:S(2)}) copy-start(f32[1,32,256]{2,1,0:T(8,128)} %copy.173) | copy-start | bytes 98308
  113.0 79.6 %copy-start.37 = (f32[1,32,256]{2,1,0:T(8,128)S(1)}, f32[1,32,256]{2,1,0:T(8,128)}, u32[]{:S(2)}) copy-start(f32[1,32,256]{2,1,0:T(8,128)} %copy.172) | copy-start | bytes 98308
  188.0 4.2 collective-permute-start.6
  189.3 6.8 collective-permute-start.7
  194.4 71.5 %copy-start.32 = (f32[128,128]{1,0:T(8,128)S(1)}, f32[128,128]{1,0:T(8,128)}, u32[]{:S(2)}) copy-start(f32[128,128]{1,0:T(8,128)} %get-tuple-element.278) | copy-start | bytes 196612
  194.4 71.5 %copy-start.33 = (f32[128,128]{1,0:T(8,128)S(1)}, f32[128,128]{1,0:T(8,128)}, u32[]{:S(2)}) copy-start(f32[128,128]{1,0:T(8,128)} %get-tuple-element.279) | copy-start | bytes 196612
  194.4 71.5 %copy-start.34 = (f32[128,128]{1,0:T(8,128)S(1)}, f32[128,128]{1,0:T(8,128)}, u32[]{:S(2)}) copy-start(f32[128,128]{1,0:T(8,128)} %fusion.331) | copy-start | bytes 196612
  194.4 71.5 %copy-start.35 = (f32[128,128]{1,0:T(8,128)S(1)}, f32[128,128]{1,0:T(8,128)}, u32[]{:S(2)}) copy-start(f32[128,128]{1,0:T(8,128)} %get-tuple-element.216) | copy-start | bytes 196612
  194.4 71.5 %copy-start.36 = (f32[128,128]{1,0:T(8,128)S(1)}, f32[128,128]{1,0:T(8,128)}, u32[]{:S(2)}) copy-start(f32[128,128]{1,0:T(8,128)} %get-tuple-element.217) | copy-start | bytes 196612
  561.4 112.8 %copy-start.31 = (f32[1024]{0:T(1024)S(1)}, f32[1024]{0:T(1024)}, u32[]{:S(2)}) copy-start(f32[1024]{0:T(1024)} %all-reduce.10) | copy-start | bytes 12292
  674.1 21.2 %copy-start.1 = (f32[8,16,32,256]{3,2,1,0:T(8,128)S(1)}, f32[8,16,32,256]{3,2,1,0:T(8,128)}, u32[]{:S(2)}) copy-start(f32[8,16,32,256]{3,2,1,0:T(8,128)} %param.9) | copy-start | bytes 12582916
  681.3 19.3 %copy-start.23 = (f32[16,32,256]{2,1,0:T(8,128)S(1)}, f32[16,32,256]{2,1,0:T(8,128)}, u32[]{:S(2)}) copy-start(f32[16,32,256]{2,1,0:T(8,128)} %param.7) | copy-start | bytes 1572868
  690.4 23.6 %copy-start.27 = (f32[16,32,256]{2,1,0:T(8,128)S(1)}, f32[16,32,256]{2,1,0:T(8,128)}, u32[]{:S(2)}) copy-start(f32[16,32,256]{2,1,0:T(8,128)} %param.6) | copy-start | bytes 1572868
  701.2 30.9 %copy-start.15 = (f32[16,32,256]{2,0,1:T(8,128)}, f32[16,32,256]{2,0,1:T(8,128)S(1)}, u32[]{:S(2)}) copy-start(f32[16,32,256]{2,0,1:T(8,128)S(1)} %bitcast_add_fusion.1) | copy-start | bytes 1572868
  701.2 5.6 collective-permute-start.12
  704.5 3.3 collective-permute-start.13
  707.8 5.3 collective-permute-start.14
  709.1 4.9 collective-permute-start.15
  716.3 26.6 %copy-start.13 = (f32[16,32,256]{2,0,1:T(8,128)}, f32[16,32,256]{2,0,1:T(8,128)S(1)}, u32[]{:S(2)}) copy-start(f32[16,32,256]{2,0,1:T(8,128)S(1)} %get-tuple-element.65) | copy-start | bytes 1572868
  716.3 7.3 collective-permute-start.16
  719.3 5.3 collective-permute-start.17
  724.6 6.0 collective-permute-start.18
  725.9 5.5 collective-permute-start.19
  813.0 21.1 %copy-start.2 = (f32[8,16,32,256]{3,2,1,0:T(8,128)S(1)}, f32[8,16,32,256]{3,2,1,0:T(8,128)}, u32[]{:S(2)}) copy-start(f32[8,16,32,256]{3,2,1,0:T(8,128)} %param.9) | copy-start | bytes 12582916
  820.1 19.2 %copy-start.14 = (f32[16,32,256]{2,0,1:T(8,128)S(1)}, f32[16,32,256]{2,0,1:T(8,128)}, u32[]{:S(2)}) copy-start(f32[16,32,256]{2,0,1:T(8,128)} %copy-done.13) | copy-start | bytes 1572868
  839.8 5.7 collective-permute-start.20
  842.3 4.1 collective-permute-start.21
  846.5 5.3 collective-permute-start.22
  847.8 5.0 collective-permute-start.23
  924.2 16.3 %copy-start.3 = (f32[8,16,32,256]{3,2,1,0:T(8,128)S(1)}, f32[8,16,32,256]{3,2,1,0:T(8,128)}, u32[]{:S(2)}) copy-start(f32[8,16,32,256]{3,2,1,0:T(8,128)} %param.9) | copy-start | bytes 12582916
  927.0 24.0 %copy-start.11 = (f32[16,32,256]{2,0,1:T(8,128)}, f32[16,32,256]{2,0,1:T(8,128)S(1)}, u32[]{:S(2)}) copy-start(f32[16,32,256]{2,0,1:T(8,128)S(1)} %get-tuple-element.60) | copy-start | bytes 1572868
  927.1 5.6 collective-permute-start.24
  929.9 3.7 collective-permute-start.25
  933.7 5.7 collective-permute-start.26
  935.0 4.9 collective-permute-start.27
  1020.8 21.2 %copy-start.4 = (f32[8,16,32,256]{3,2,1,0:T(8,128)S(1)}, f32[8,16,32,256]{3,2,1,0:T(8,128)}, u32[]{:S(2)}) copy-start(f32[8,16,32,256]{3,2,1,0:T(8,128)} %param.9) | copy-start | bytes 12582916
  1028.0 19.3 %copy-start.8 = (f32[16,32,256]{2,0,1:T(8,128)S(1)}, f32[16,32,256]{2,0,1:T(8,128)}, u32[]{:S(2)}) copy-start(f32[16,32,256]{2,0,1:T(8,128)} %copy-done.7) | copy-start | bytes 1572868
  1028.0 19.3 %copy-start.12 = (f32[16,32,256]{2,0,1:T(8,128)S(1)}, f32[16,32,256]{2,0,1:T(8,128)}, u32[]{:S(2)}) copy-start(f32[16,32,256]{2,0,1:T(8,128)} %copy-done.11) | copy-start | bytes 1572868
  1047.8 5.6 collective-permute-start.28
  1050.5 3.9 collective-permute-start.29
  1054.3 5.3 collective-permute-start.30
  1055.6 4.9 collective-permute-start.31
  1134.3 24.4 %copy-start.19 = (f32[16,32,256]{2,0,1:T(8,128)}, f32[16,32,256]{2,0,1:T(8,128)S(1)}, u32[]{:S(2)}) copy-start(f32[16,32,256]{2,0,1:T(8,128)S(1)} %get-tuple-element.55) | copy-start | bytes 1572868
  1134.4 5.6 collective-permute-start.32
  1137.2 3.7 collective-permute-start.33
  1141.0 6.6 collective-permute-start.34
  1142.3 5.3 collective-permute-start.35
  1228.4 21.3 %copy-start.6 = (f32[8,16,32,256]{3,2,1,0:T(8,128)S(1)}, f32[8,16,32,256]{3,2,1,0:T(8,128)}, u32[]{:S(2)}) copy-start(f32[8,16,32,256]{3,2,1,0:T(8,128)} %param.9) | copy-start | bytes 12582916
  1235.5 19.4 %copy-start.9 = (f32[16,32,256]{2,0,1:T(8,128)S(1)}, f32[16,32,256]{2,0,1:T(8,128)}, u32[]{:S(2)}) copy-start(f32[16,32,256]{2,0,1:T(8,128)} %copy-done.7) | copy-start | bytes 1572868
  1235.5 19.4 %copy-start.16 = (f32[16,32,256]{2,0,1:T(8,128)S(1)}, f32[16,32,256]{2,0,1:T(8,128)}, u32[]{:S(2)}) copy-start(f32[16,32,256]{2,0,1:T(8,128)} %copy-done.15) | copy-start | bytes 1572868
  1235.5 19.4 %copy-start.18 = (f32[16,32,256]{2,0,1:T(8,128)S(1)}, f32[16,32,256]{2,0,1:T(8,128)}, u32[]{:S(2)}) copy-start(f32[16,32,256]{2,0,1:T(8,128)} %copy-done.17) | copy-start | bytes 1572868
  1235.5 19.4 %copy-start.20 = (f32[16,32,256]{2,0,1:T(8,128)S(1)}, f32[16,32,256]{2,0,1:T(8,128)}, u32[]{:S(2)}) copy-start(f32[16,32,256]{2,0,1:T(8,128)} %copy-done.19) | copy-start | bytes 1572868
  (14 other events, 133.6 us)
where the time goes:
time: 1270 us; the launch traced here: 1260 us
  blocking collectives  484 us (38%)
  other arithmetic  334 us (26%)
  matrix products  192 us (15%)
  local copies, waits for them, and re-layouts  126 us (10%)
  starting transfers between devices  97.7 us (8%)
  between operations  13.1 us (1%)
    unnamed x4, blocking collectives  278 us
    another operation x31, other arithmetic, per_device(): factor = jnp.linalg.cholesky(matrix)  173 us
    another operation x4, other arithmetic, solve_coarse(): solved = jax.scipy.linalg.cho_solve((factor, True), flattened)  85.2 us
    another operation x120, matrix products, solve_coarse(): solved = jax.scipy.linalg.cho_solve((factor, True), flattened)  83.1 us
    all_gather x1, blocking collectives, per_device(): gathered = lax.all_gather(blocks, ('gx', 'gy'), axis=0, tiled=True)  69.1 us
    psum x1, blocking collectives, coarse_with(): inner_sum = lax.psum(jnp.sum(residual_now * precond_now), ('gx', 'gy'))  68.3 us
    psum x1, blocking collectives, per_device(): step_size = inner_now / lax.psum(jnp.sum(direction * applied), ('gx', 'gy'))  68.1 us
    ppermute x18, starting transfers between devices, extended(): lax.ppermute(tail, axis, [(i, (i + 1) % count) for i in range(ends)])  63.2 us
  transfers between devices with their start and end apart: 36, of which 12 were waited for; matrix products, arithmetic and copies ran while one was open for 7% of the time, Pallas kernels for 0%

commit v1 on v0

--- a/solution.py
+++ b/solution.py
@@ -105,7 +105,9 @@
     above_rows = face_product(deflation[:, -1], face_rows[-1], rimmed[:, -1, 1:-1])
     above_cols = face_product(deflation[:, :, -1], face_cols[:, -1], rimmed[:, 1:-1, -1])
     blocks = jnp.stack([diag_block, below_rows, below_cols, above_rows, above_cols])[None]
-    gathered = lax.all_gather(blocks, ("gx", "gy"), axis=0, tiled=True)
+    q_next = jnp.stack(tuple((blocks for _ in range(lax.axis_size(("gx", "gy"))))))
+    last = lax.all_to_all(q_next, ("gx", "gy"), 0, 0)
+    gathered = jnp.concatenate(last, 0)
     self_mask, mask_below_rows, mask_below_cols, mask_above_rows, mask_above_cols = block_masks(
         block_count, across
     )

time: 1270 us -> 1230 us (0.969)
  blocking collectives: 484 us -> 410 us
  starting transfers between devices: 97.7 us -> 119 us
    all_gather x1 -> x0, blocking collectives: 69.1 us -> none  [per_device(): gathered = lax.all_gather(blocks, ('gx', 'gy'), axis=0, tiled=True)]
    all_to_all x0 -> x1, starting transfers between devices: none -> 19.2 us  [per_device(): last = lax.all_to_all(q_next, ('gx', 'gy'), 0, 0)]
  transfers between devices with their start and end apart: 36 -> 37, of which waited for: 12 -> 12; matrix products, arithmetic and copies ran while one was open for 7% -> 7% of each run, Pallas kernels for 0% -> 0%
where the time goes in v1:
time: 1230 us; the launch traced here: 1210 us
  blocking collectives  410 us (33%)
  other arithmetic  334 us (27%)
  matrix products  190 us (15%)
  local copies, waits for them, and re-layouts  134 us (11%)
  starting transfers between devices  119 us (10%)
  between operations  12.8 us (1%)
    unnamed x4, blocking collectives  274 us
    another operation x31, other arithmetic, per_device(): factor = jnp.linalg.cholesky(matrix)  173 us
    another operation x4, other arithmetic, solve_coarse(): solved = jax.scipy.linalg.cho_solve((factor, True), flattened)  85.2 us
    another operation x120, matrix products, solve_coarse(): solved = jax.scipy.linalg.cho_solve((factor, True), flattened)  83.1 us
    psum x1, blocking collectives, coarse_with(): inner_sum = lax.psum(jnp.sum(residual_now * precond_now), ('gx', 'gy'))  68 us
    psum x1, blocking collectives, per_device(): step_size = inner_now / lax.psum(jnp.sum(direction * applied), ('gx', 'gy'))  67.9 us
    ppermute x18, starting transfers between devices, extended(): lax.ppermute(tail, axis, [(i, (i + 1) % count) for i in range(ends)])  65.7 us
    add x2, local copies, waits for them, and re-layouts, per_device(): matrix + place(mask_above_rows, gathered[:, 3])  53.8 us
  transfers between devices with their start and end apart: 37, of which 12 were waited for; matrix products, arithmetic and copies ran while one was open for 7% of the time, Pallas kernels for 0%

profile of v1, /device:TPU:1, one launch (start us, length us, event | category | flops | bytes accessed | tf_op | source)
XLA Modules:
  0.0 1211.3 jit_solution(13465531051411022679)
XLA Ops:
  2.1 4.6 collective-permute-start
  13.2 3.9 collective-permute-start.9
  17.1 5.5 copy.71
  31.5 4.5 copy.73
  46.8 3.1 collective-permute-start.2
  56.7 4.6 collective-permute-start.11
  68.2 14.7 %fusion.6 = f32[8,16,32,256]{3,2,1,0:T(8,128)} fusion(f32[8,16,32,256]{3,2,1,0:T(8,128)} %param.9, f32[16,32,256]{2,1,0:T(8,128)} %copy.69, f32[16,32,256]{2,1,0:T(8,128)} %copy.68, f32[16,32,256]{2,1,0:T(8,128)} %copy.67, f32[16,32,256]{2,1,0:T(8,128)} %copy.66, f32[16,32,256]{2,1,0:T(8,128)} %copy.65, f32[16,32,256]{2,1,0:T(8,128)} %copy.64, ...), kind=kLoop, calls=%fused_computation.16 | loop fusion | flops 13631488 | bytes 12058624 | tf_op jit(solution)/shard_map/sub | solution.py:49
  83.0 15.2 %fusion.15 = f32[8,8]{0,1:T(8,128)S(1)} fusion(f32[8,16,32,256]{3,2,1,0:T(8,128)} %fusion.6, f32[8,16,32,256]{3,2,1,0:T(8,128)} %param.9), kind=kOutput, calls=%fused_computation.42 | convolution fusion | flops 100663296 | bytes 8388864 | tf_op jit(solution)/shard_map/kxyz,lxyz->kl/dot_general | solution.py:101
  99.4 3.5 collective-permute-start.6
  111.5 3.7 reshape.876
  115.1 19.2 %all-to-all-start = ((f32[128,1,320]{2,1,0:T(1,128)}), f32[128,1,320]{2,1,0:T(1,128)S(1)}, u32[]{:S(2)}, u32[]{:S(2)}) async-start(f32[128,1,320]{2,1,0:T(1,128)} %reshape.876), calls=%async_computation | async-start | bytes 393216 | tf_op jit(solution)/shard_map/all_to_all | solution.py:109
  134.4 12.0 convolution_bitcast_fusion.23
  146.6 67.1 %all-reduce.10 = f32[1024]{0:T(1024)S(1)} all-reduce(f32[1024]{0:T(1024)S(1)} %dynamic-update-slice.50), channel_id=2, replica_groups=mesh['gx'=8,'gy'=16] {'gx','gy'}, use_global_device_ids=true, to_apply=%add.10 | all-reduce | flops 1024 | bytes 8192
  219.7 31.1 %multiply_add_fusion = f32[128,8,128,8]{3,2,1,0:T(8,128)} fusion(f32[128,8,8]{2,1,0:T(8,128)S(1)} %get-tuple-element.76, f32[128,128]{1,0:T(8,128)S(1)} %copy-done.35, f32[128,8,8]{2,1,0:T(8,128)S(1)} %get-tuple-element.77, f32[128,128]{1,0:T(8,128)S(1)} %copy-done.33, f32[128,8,8]{2,1,0:T(8,128)S(1)} %get-tuple-element.78, f32[128,128]{1,0:T(8,128)S(1)} %copy-done.34, ...), kind=kLoop, calls=%fused_computation.2 | loop fusion | flops 9437184 | bytes 4685824 | tf_op jit(solution)/shard_map/add | solution.py:120
  250.8 48.3 %reshape.514 = f32[1024,1024]{1,0:T(8,128)} reshape(f32[128,8,128,8]{3,2,1,0:T(8,128)} %multiply_add_fusion) | data formatting | bytes 8388608 | tf_op jit(solution)/shard_map/add | solution.py:120
  299.1 5.5 copy.81
  304.6 4.4 fusion.12
  311.1 11.7 cholesky.226
  325.4 9.8 custom-call.64
  339.1 11.9 cholesky.247
  352.9 9.8 custom-call.65
  366.1 11.7 cholesky.474
  379.1 9.8 custom-call.66
  392.4 12.1 cholesky.493
  405.8 9.8 custom-call.67
  419.1 11.7 cholesky.512
  432.1 9.9 custom-call.68
  445.3 11.7 cholesky.532
  458.3 9.8 custom-call.69
  471.2 11.9 cholesky.552
  484.4 9.8 custom-call.70
  496.8 11.7 cholesky.570
  514.9 4.9 select_select_fusion
  519.7 28.0 %while.8 = (s32[]{:T(128)}, f32[1024,1024]{1,0:T(8,128)}, s32[8,2]{0,1:T(2,128)S(1)}, f32[8,128,128]{2,1,0:T(8,128)}, s32[]{:T(128)}) while((s32[]{:T(128)}, f32[1024,1024]{1,0:T(8,128)}, s32[8,2]{0,1:T(2,128)S(1)}, f32[8,128,128]{2,1,0:T(8,128)}, s32[]{:T(128)}) %tuple.176), condition=%wide.while_cond, body=%wide.while_body.sunk | while | flops 2 | bytes 132705 | solution.py:127
  520.3 2.9 bitcast_dynamic-update-slice_fusion.2
  523.8 2.9 bitcast_dynamic-update-slice_fusion.2
  527.4 2.9 bitcast_dynamic-update-slice_fusion.2
  530.9 2.9 bitcast_dynamic-update-slice_fusion.2
  534.4 2.9 bitcast_dynamic-update-slice_fusion.2
  537.9 2.9 bitcast_dynamic-update-slice_fusion.2
  541.4 2.9 bitcast_dynamic-update-slice_fusion.2
  544.9 2.8 bitcast_dynamic-update-slice_fusion.2
  547.8 79.8 %custom-call.74 = f32[8,128,128]{1,2,0:T(8,128)S(1)} custom-call(f32[8,128,128]{2,1,0:T(8,128)} %get-tuple-element.30), custom_call_target="InvertDiagBlocksLowerTriangular" | custom-call | tf_op jit(solution)/shard_map/jit(_cho_solve)/triangular_solve | solution.py:127
  648.8 5.2 fusion.497
  662.6 4.0 collective-permute-start.15
  672.4 4.8 collective-permute-start.17
  679.5 4.7 collective-permute-start.19
  685.6 10.9 convolution_bitcast_fusion.18
  696.7 70.0 %all-reduce.11 = f32[1024]{0:T(1024)S(1)} all-reduce(f32[1024]{0:T(1024)S(1)} %dynamic-update-slice.51), channel_id=3, replica_groups=mesh['gx'=8,'gy'=16] {'gx','gy'}, use_global_device_ids=true, to_apply=%add.11 | all-reduce | flops 1024 | bytes 8192
  787.8 5.2 fusion.495
  793.4 3.0 collective-permute-start.20
  801.3 4.0 collective-permute-start.23
  808.2 68.0 %all-reduce.16 = (f32[]{:T(128)}, f32[]{:T(128)}) all-reduce(f32[]{:T(128)} %get-tuple-element.64, f32[]{:T(128)} %get-tuple-element.62), channel_id=1, replica_groups=mesh['gx'=8,'gy'=16] {'gx','gy'}, use_global_device_ids=true, to_apply=%region_17.19 | all-reduce | flops 2 | bytes 16 | tf_op jit(solution)/shard_map/psum | solution.py:141
  877.4 3.0 multiply_reduce_fusion.2
  888.3 4.4 collective-permute-start.27
  893.8 10.6 convolution_bitcast_fusion.13
  904.6 68.5 %all-reduce.15 = (f32[1024]{0:T(1024)S(1)}, f32[]{:T(128)}) all-reduce(f32[1024]{0:T(1024)S(1)} %dynamic-update-slice.52, f32[]{:T(128)} %get-tuple-element.59), channel_id=4, replica_groups=mesh['gx'=8,'gy'=16] {'gx','gy'}, use_global_device_ids=true, to_apply=%add.12 | all-reduce | flops 1025 | bytes 8200
  995.7 5.2 fusion.493
  1009.3 4.0 collective-permute-start.31
  1016.2 67.9 %psum.38 = f32[]{:T(128)} all-reduce(f32[]{:T(128)} %get-tuple-element.57), channel_id=1, replica_groups=mesh['gx'=8,'gy'=16] {'gx','gy'}, use_global_device_ids=true, to_apply=%region_23.25 | all-reduce | flops 1 | bytes 8 | tf_op jit(solution)/shard_map/psum | solution.py:151
  1095.6 4.2 collective-permute-start.35
  1101.5 10.6 convolution_bitcast_fusion.8
  1112.4 68.1 %all-reduce.14 = (f32[1024]{0:T(1024)S(1)}, f32[]{:T(128)}) all-reduce(f32[1024]{0:T(1024)S(1)} %dynamic-update-slice.53, f32[]{:T(128)} %get-tuple-element.54), channel_id=5, replica_groups=mesh['gx'=8,'gy'=16] {'gx','gy'}, use_global_device_ids=true, to_apply=%add.13 | all-reduce | flops 1025 | bytes 8200
  1203.0 5.2 fusion.491
  (494 shorter events, 244.9 us)
Async XLA Ops:
  2.1 42.5 %collective-permute-start = (f32[1,32,256]{2,0,1:T(1,128)}, f32[1,32,256]{2,0,1:T(1,128)}, u32[]{:S(2)}, u32[]{:S(2)}) collective-permute-start(f32[1,32,256]{2,0,1:T(1,128)} %copy.57), channel_id=1, source_target_pairs={{0,16},{16,32},{32,48},{48,64},{64,80},{80,96},{96,112},{1,17},{17... | collective-permute-start | bytes 98312 | tf_op jit(solution)/shard_map/ppermute | solution.py:18
  7.3 33.6 %collective-permute-start.1 = (f32[1,32,256]{2,0,1:T(1,128)}, f32[1,32,256]{2,0,1:T(1,128)}, u32[]{:S(2)}, u32[]{:S(2)}) collective-permute-start(f32[1,32,256]{2,0,1:T(1,128)} %copy.59), channel_id=1, source_target_pairs={{16,0},{32,16},{48,32},{64,48},{80,64},{96,80},{112,96},{17,1},{33... | collective-permute-start | bytes 98312 | tf_op jit(solution)/shard_map/ppermute | solution.py:20
  10.6 39.3 %collective-permute-start.8 = (f32[1,32,256]{2,0,1:T(1,128)}, f32[1,32,256]{2,0,1:T(1,128)}, u32[]{:S(2)}, u32[]{:S(2)}) collective-permute-start(f32[1,32,256]{2,0,1:T(1,128)} %copy.83), channel_id=1, source_target_pairs={{16,0},{32,16},{48,32},{64,48},{80,64},{96,80},{112,96},{17,1},{33... | collective-permute-start | bytes 98312 | tf_op jit(solution)/shard_map/ppermute | solution.py:20
  13.2 12.9 %copy-start = (f32[8,16,32,256]{3,2,1,0:T(8,128)S(1)}, f32[8,16,32,256]{3,2,1,0:T(8,128)}, u32[]{:S(2)}) copy-start(f32[8,16,32,256]{3,2,1,0:T(8,128)} %param.9) | copy-start | bytes 12582916
  13.2 38.0 %collective-permute-start.9 = (f32[1,32,256]{2,0,1:T(1,128)}, f32[1,32,256]{2,0,1:T(1,128)}, u32[]{:S(2)}, u32[]{:S(2)}) collective-permute-start(f32[1,32,256]{2,0,1:T(1,128)} %copy.85), channel_id=1, source_target_pairs={{0,16},{16,32},{32,48},{48,64},{64,80},{80,96},{96,112},{1,17},{17... | collective-permute-start | bytes 98312 | tf_op jit(solution)/shard_map/ppermute | solution.py:18
  23.3 75.0 %collective-permute-start.4 = (f32[8,1,32,256]{3,0,2,1:T(8,128)}, f32[8,1,32,256]{3,0,2,1:T(8,128)S(1)}, u32[]{:S(2)}, u32[]{:S(2)}) collective-permute-start(f32[8,1,32,256]{3,0,2,1:T(8,128)} %slice.817), channel_id=1, source_target_pairs={{0,16},{16,32},{32,48},{48,64},{64,80},{80,96},{96,112},{1,17},{17... | collective-permute-start | bytes 786440 | tf_op jit(solution)/shard_map/ppermute | solution.py:18
  40.9 57.5 %collective-permute-start.5 = (f32[8,1,32,256]{3,0,1,2:T(8,128)}, f32[8,1,32,256]{3,0,1,2:T(8,128)}, u32[]{:S(2)}, u32[]{:S(2)}) collective-permute-start(f32[8,1,32,256]{3,0,1,2:T(8,128)} %slice.815), channel_id=1, source_target_pairs={{16,0},{32,16},{48,32},{64,48},{80,64},{96,80},{112,96},{17,1},{33... | collective-permute-start | bytes 786440 | tf_op jit(solution)/shard_map/ppermute | solution.py:20
  46.0 17.2 %copy-start.26 = (f32[16,32,256]{2,1,0:T(8,128)S(1)}, f32[16,32,256]{2,1,0:T(8,128)}, u32[]{:S(2)}) copy-start(f32[16,32,256]{2,1,0:T(8,128)} %param.6) | copy-start | bytes 1572868
  46.8 9.9 collective-permute-start.2
  49.9 11.4 collective-permute-start.3
  52.0 11.2 collective-permute-start.10
  56.7 6.4 collective-permute-start.11
  83.0 15.3 %copy-start.30 = (f32[8,16,1,256]{3,2,1,0:T(1,128)S(1)}, f32[8,16,1,256]{3,2,1,0:T(1,128)}, u32[]{:S(2)}) copy-start(f32[8,16,1,256]{3,2,1,0:T(1,128)} %get-tuple-element.74) | copy-start | bytes 393220
  83.0 15.3 %copy-start.39 = (f32[16,256]{1,0:T(8,128)S(1)}, f32[16,256]{1,0:T(8,128)}, u32[]{:S(2)}) copy-start(f32[16,256]{1,0:T(8,128)} %get-tuple-element.103) | copy-start | bytes 49156
  83.0 15.3 %copy-start.38 = (f32[16,256]{1,0:T(8,128)S(1)}, f32[16,256]{1,0:T(8,128)}, u32[]{:S(2)}) copy-start(f32[16,256]{1,0:T(8,128)} %get-tuple-element.102) | copy-start | bytes 49156
  99.4 35.0 %copy-start.28 = (f32[16,32,256,1]{2,0,1,3:T(8,128)S(1)}, f32[16,32,256,1]{2,0,1,3:T(8,128)}, u32[]{:S(2)}) copy-start(f32[16,32,256,1]{2,0,1,3:T(8,128)} %get-tuple-element.67) | copy-start | bytes 1572868
  99.4 6.8 collective-permute-start.6
  102.9 6.5 collective-permute-start.7
  115.1 98.6 %all-to-all-start = ((f32[128,1,320]{2,1,0:T(1,128)}), f32[128,1,320]{2,1,0:T(1,128)S(1)}, u32[]{:S(2)}, u32[]{:S(2)}) async-start(f32[128,1,320]{2,1,0:T(1,128)} %reshape.876), calls=%async_computation | async-start | bytes 393216 | tf_op jit(solution)/shard_map/all_to_all | solution.py:109
  627.6 21.2 %copy-start.1 = (f32[8,16,32,256]{3,2,1,0:T(8,128)S(1)}, f32[8,16,32,256]{3,2,1,0:T(8,128)}, u32[]{:S(2)}) copy-start(f32[8,16,32,256]{3,2,1,0:T(8,128)} %param.9) | copy-start | bytes 12582916
  634.7 19.3 %copy-start.23 = (f32[16,32,256]{2,1,0:T(8,128)S(1)}, f32[16,32,256]{2,1,0:T(8,128)}, u32[]{:S(2)}) copy-start(f32[16,32,256]{2,1,0:T(8,128)} %param.7) | copy-start | bytes 1572868
  643.9 23.6 %copy-start.27 = (f32[16,32,256]{2,1,0:T(8,128)S(1)}, f32[16,32,256]{2,1,0:T(8,128)}, u32[]{:S(2)}) copy-start(f32[16,32,256]{2,1,0:T(8,128)} %param.6) | copy-start | bytes 1572868
  654.6 31.0 %copy-start.15 = (f32[16,32,256]{2,0,1:T(8,128)}, f32[16,32,256]{2,0,1:T(8,128)S(1)}, u32[]{:S(2)}) copy-start(f32[16,32,256]{2,0,1:T(8,128)S(1)} %bitcast_add_fusion.1) | copy-start | bytes 1572868
  654.7 5.6 collective-permute-start.12
  657.5 3.8 collective-permute-start.13
  661.3 5.3 collective-permute-start.14
  662.6 4.9 collective-permute-start.15
  669.8 26.6 %copy-start.13 = (f32[16,32,256]{2,0,1:T(8,128)}, f32[16,32,256]{2,0,1:T(8,128)S(1)}, u32[]{:S(2)}) copy-start(f32[16,32,256]{2,0,1:T(8,128)S(1)} %get-tuple-element.65) | copy-start | bytes 1572868
  669.9 7.3 collective-permute-start.16
  672.4 5.8 collective-permute-start.17
  678.2 6.0 collective-permute-start.18
  679.5 5.5 collective-permute-start.19
  766.7 21.1 %copy-start.2 = (f32[8,16,32,256]{3,2,1,0:T(8,128)S(1)}, f32[8,16,32,256]{3,2,1,0:T(8,128)}, u32[]{:S(2)}) copy-start(f32[8,16,32,256]{3,2,1,0:T(8,128)} %param.9) | copy-start | bytes 12582916
  773.8 19.2 %copy-start.14 = (f32[16,32,256]{2,0,1:T(8,128)S(1)}, f32[16,32,256]{2,0,1:T(8,128)}, u32[]{:S(2)}) copy-start(f32[16,32,256]{2,0,1:T(8,128)} %copy-done.13) | copy-start | bytes 1572868
  793.4 12.9 %copy-start.7 = (f32[16,32,256]{2,0,1:T(8,128)}, f32[16,32,256]{2,0,1:T(8,128)S(1)}, u32[]{:S(2)}) copy-start(f32[16,32,256]{2,0,1:T(8,128)S(1)} %bitcast_subtract_fusion.2) | copy-start | bytes 1572868
  793.4 5.6 collective-permute-start.20
  796.5 3.6 collective-permute-start.21
  800.0 5.3 collective-permute-start.22
  801.3 4.9 collective-permute-start.23
  877.4 16.4 %copy-start.3 = (f32[8,16,32,256]{3,2,1,0:T(8,128)S(1)}, f32[8,16,32,256]{3,2,1,0:T(8,128)}, u32[]{:S(2)}) copy-start(f32[8,16,32,256]{3,2,1,0:T(8,128)} %param.9) | copy-start | bytes 12582916
  880.4 24.0 %copy-start.11 = (f32[16,32,256]{2,0,1:T(8,128)}, f32[16,32,256]{2,0,1:T(8,128)S(1)}, u32[]{:S(2)}) copy-start(f32[16,32,256]{2,0,1:T(8,128)S(1)} %get-tuple-element.60) | copy-start | bytes 1572868
  880.4 5.6 collective-permute-start.24
  883.3 3.7 collective-permute-start.25
  887.0 5.7 collective-permute-start.26
  888.3 4.9 collective-permute-start.27
  974.5 21.2 %copy-start.4 = (f32[8,16,32,256]{3,2,1,0:T(8,128)S(1)}, f32[8,16,32,256]{3,2,1,0:T(8,128)}, u32[]{:S(2)}) copy-start(f32[8,16,32,256]{3,2,1,0:T(8,128)} %param.9) | copy-start | bytes 12582916
  981.6 19.3 %copy-start.8 = (f32[16,32,256]{2,0,1:T(8,128)S(1)}, f32[16,32,256]{2,0,1:T(8,128)}, u32[]{:S(2)}) copy-start(f32[16,32,256]{2,0,1:T(8,128)} %copy-done.7) | copy-start | bytes 1572868
  981.6 19.3 %copy-start.12 = (f32[16,32,256]{2,0,1:T(8,128)S(1)}, f32[16,32,256]{2,0,1:T(8,128)}, u32[]{:S(2)}) copy-start(f32[16,32,256]{2,0,1:T(8,128)} %copy-done.11) | copy-start | bytes 1572868
  1001.3 12.9 %copy-start.17 = (f32[16,32,256]{2,0,1:T(8,128)}, f32[16,32,256]{2,0,1:T(8,128)S(1)}, u32[]{:S(2)}) copy-start(f32[16,32,256]{2,0,1:T(8,128)S(1)} %bitcast_subtract_fusion.1) | copy-start | bytes 1572868
  1001.4 5.6 collective-permute-start.28
  1004.2 3.8 collective-permute-start.29
  1008.0 5.3 collective-permute-start.30
  1009.3 4.9 collective-permute-start.31
  1085.5 16.0 %copy-start.5 = (f32[8,16,32,256]{3,2,1,0:T(8,128)S(1)}, f32[8,16,32,256]{3,2,1,0:T(8,128)}, u32[]{:S(2)}) copy-start(f32[8,16,32,256]{3,2,1,0:T(8,128)} %param.9) | copy-start | bytes 12582916
  1087.7 24.4 %copy-start.19 = (f32[16,32,256]{2,0,1:T(8,128)}, f32[16,32,256]{2,0,1:T(8,128)S(1)}, u32[]{:S(2)}) copy-start(f32[16,32,256]{2,0,1:T(8,128)S(1)} %get-tuple-element.55) | copy-start | bytes 1572868
  1087.8 5.6 collective-permute-start.32
  1090.6 3.7 collective-permute-start.33
  1094.3 6.6 collective-permute-start.34
  1095.6 5.3 collective-permute-start.35
  1181.7 21.3 %copy-start.6 = (f32[8,16,32,256]{3,2,1,0:T(8,128)S(1)}, f32[8,16,32,256]{3,2,1,0:T(8,128)}, u32[]{:S(2)}) copy-start(f32[8,16,32,256]{3,2,1,0:T(8,128)} %param.9) | copy-start | bytes 12582916
  1188.8 19.4 %copy-start.9 = (f32[16,32,256]{2,0,1:T(8,128)S(1)}, f32[16,32,256]{2,0,1:T(8,128)}, u32[]{:S(2)}) copy-start(f32[16,32,256]{2,0,1:T(8,128)} %copy-done.7) | copy-start | bytes 1572868
  1188.8 19.4 %copy-start.16 = (f32[16,32,256]{2,0,1:T(8,128)S(1)}, f32[16,32,256]{2,0,1:T(8,128)}, u32[]{:S(2)}) copy-start(f32[16,32,256]{2,0,1:T(8,128)} %copy-done.15) | copy-start | bytes 1572868
  1188.8 19.4 %copy-start.18 = (f32[16,32,256]{2,0,1:T(8,128)S(1)}, f32[16,32,256]{2,0,1:T(8,128)}, u32[]{:S(2)}) copy-start(f32[16,32,256]{2,0,1:T(8,128)} %copy-done.17) | copy-start | bytes 1572868
  1188.9 19.4 %copy-start.20 = (f32[16,32,256]{2,0,1:T(8,128)S(1)}, f32[16,32,256]{2,0,1:T(8,128)}, u32[]{:S(2)}) copy-start(f32[16,32,256]{2,0,1:T(8,128)} %copy-done.19) | copy-start | bytes 1572868
  (14 other events, 81.4 us)
